TPU v7x, 512 devices: a whole 4x4x16 slice. The times are simulated.
512 devices in a mesh: seq: 32 (over z, core), mp: 16 (over y, x).
Axes of the slice: x: 4, y: 4, z: 16, core: 2. Of those that a mesh axis runs over, the one named last changes fastest.
Arguments:
- continued_prompt_entries: bfloat16 [4096, 4096], P('seq', 'mp'), may hold values from -6 to 6
- padded_prompt_entries: bfloat16 [4096, 4096], P('seq', 'mp'), may hold values from -6 to 6
- prompt_live_extents: int32 [64], P('seq'), may hold values from 8 to 64, as said below
- preceding_entry_line: bfloat16 [4096], P('mp'), may hold values from -6 to 6
- carried_memory: float32 [64, 64, 64], P('mp'), may hold values from -24 to 24
- token_mixing_ratios: float32 [5, 4096], replicated, may hold values from 0.05 to 0.95
- acceptance_transform: bfloat16 [4096, 4096], P('seq', 'mp'), may hold values from -0.09375 to 0.09375
- lookup_transform: bfloat16 [4096, 4096], P('seq', 'mp'), may hold values from -0.09375 to 0.09375
- payload_transform: bfloat16 [4096, 4096], P('seq', 'mp'), may hold values from -0.09375 to 0.09375
- gating_transform: bfloat16 [4096, 4096], P('seq', 'mp'), may hold values from -0.09375 to 0.09375
- fading_baseline: float32 [4096], P('mp'), may hold values from -10 to -3.5
- fading_left_factor: bfloat16 [4096, 128], replicated, may hold values from -0.09375 to 0.09375
- fading_right_factor: bfloat16 [128, 4096], P(None, 'mp'), may hold values from -0.5 to 0.5
- present_reward: float32 [64, 64], P('mp'), may hold values from -3 to 3
- group_layer_scaling: float32 [4096], P('mp'), may hold values from 0.5 to 1.5
- group_layer_shift_term: float32 [4096], P('mp'), may hold values from -1.8 to 1.8
- final_transform: bfloat16 [4096, 4096], P('mp', 'seq'), may hold values from -0.09375 to 0.09375
Outputs:
- mixed: bfloat16 [32, 256, 4096], P('seq', 'mp')
- span_states: float32 [32, 64, 64, 64], P('seq', 'mp')
- request_states: float32 [64, 64, 64, 64], P('seq', 'mp')
Inputs may be any that keep to these rules, and one draw needn't show every extreme that they name: `prompt_live_extents`: some request has all 64 rows live.
All inputs are finite; a program needn't handle non-finite values.
Results may differ from a plain program's by a relative error of at most 0.0076.
Values may be sent and summed in bfloat16 or wider, within the bound.
A program may use at most 64 MiB of HBM per device.

v0:
```python
import jax
import jax.numpy as jnp
from jax import lax
from jax.sharding import PartitionSpec as P

BLK = 64
SEQ = ("z", "core")
norm_eps = 0.00064
highest = lax.Precision.HIGHEST


def seq_index():
    return lax.axis_index("z") * lax.axis_size("core") + lax.axis_index("core")


def seq_shift(x, by, length):
    pairs = [(i, i + by) for i in range(length) if i + by < length]
    return lax.ppermute(x, SEQ, pairs)


def exclusive_prefix(value, start, length):
    mine = seq_index()
    arrived = seq_shift(value, 1, length)
    total = jax.tree.map(lambda got, first: jnp.where(mine == 0, first, got), arrived, start)
    step = 1
    while step < length:
        got = seq_shift(total, step, length)
        joined = combine(got, total)
        total = jax.tree.map(lambda new, old: jnp.where(mine >= step, new, old), joined, total)
        step *= 2
    return total


def mix_rows(current, previous, weight):
    here = current.astype(jnp.float32)
    return (here + weight[None, :] * (previous.astype(jnp.float32) - here)).astype(jnp.bfloat16)


def block_sweep(
    evolving_memory,
    acceptance_entries,
    lookup_entries,
    payload_entries,
    log_fading_amount,
    diagonal_reward,
):
    inclusive = jnp.cumsum(log_fading_amount, axis=0)
    exclusive = inclusive - log_fading_amount
    recept_scaled = acceptance_entries * jnp.exp(exclusive)
    keys_scaled = lookup_entries * jnp.exp(-inclusive)
    scores = jnp.einsum("ihc,jhc->hij", recept_scaled, keys_scaled, precision=highest)
    count = acceptance_entries.shape[0]
    row_index = lax.broadcasted_iota(jnp.int32, (count, count), 0)
    col_index = lax.broadcasted_iota(jnp.int32, (count, count), 1)
    scores = jnp.where((row_index > col_index)[None], scores, 0.0)
    diagonal_contribution = jnp.sum(
        acceptance_entries * diagonal_reward[None] * lookup_entries, axis=-1, keepdims=True
    )
    answer_lines = (
        jnp.einsum("hij,jhd->ihd", scores, payload_entries, precision=highest)
        + diagonal_contribution * payload_entries
    )
    answer_lines = answer_lines + jnp.einsum(
        "ihc,hcd->ihd", recept_scaled, evolving_memory, precision=highest
    )
    total = inclusive[-1]
    carried = lookup_entries * jnp.exp(total[None] - inclusive)
    new_state = jnp.exp(total)[:, :, None] * evolving_memory + jnp.einsum(
        "jhc,jhd->hcd", carried, payload_entries, precision=highest
    )
    return (new_state, answer_lines)


def continued_recurrence(
    acceptance_entries, lookup_entries, payload_entries, log_fading_amount, diagonal_reward
):
    length, per_group_view, embedding_dimension = acceptance_entries.shape
    blocks = length // BLK

    def step(evolving_memory, entry_lines):
        return block_sweep(
            evolving_memory,
            entry_lines[0],
            entry_lines[1],
            entry_lines[2],
            entry_lines[3],
            diagonal_reward,
        )

    shaped = tuple(
        (
            a.reshape(blocks, BLK, per_group_view, embedding_dimension)
            for a in (acceptance_entries, lookup_entries, payload_entries, log_fading_amount)
        )
    )
    evolving_memory, results = lax.scan(
        step,
        jnp.zeros((per_group_view, embedding_dimension, embedding_dimension), jnp.float32),
        shaped,
    )
    return (evolving_memory, results.reshape(length, per_group_view, embedding_dimension))


def combine(earlier, later):
    return (earlier[0] + later[0], jnp.exp(later[0])[:, :, None] * earlier[1] + later[1])


def shifted_rows(current, edge_row, long_rows, requests, slot_rows):
    feature_part = current.shape[1]
    long_prev = jnp.concatenate([edge_row, current[: long_rows - 1]], axis=0)
    short_view = current[long_rows:].reshape(requests, slot_rows, feature_part)
    short_prev = jnp.concatenate(
        [jnp.zeros((requests, 1, feature_part), current.dtype), short_view[:, :-1]], axis=1
    )
    short_prev = short_prev.reshape(requests * slot_rows, feature_part)
    return jnp.concatenate([long_prev, short_prev], axis=0)


def on_device(
    continued_prompt_entries,
    padded_prompt_entries,
    prompt_live_extents,
    preceding_entry_line,
    carried_memory,
    token_mixing_ratios,
    acceptance_transform,
    lookup_transform,
    payload_transform,
    gating_transform,
    fading_baseline,
    fading_left_factor,
    fading_right_factor,
    present_reward,
    group_layer_scaling,
    group_layer_shift_term,
    final_transform,
):
    long_rows = continued_prompt_entries.shape[0]
    requests = prompt_live_extents.shape[0]
    slot_rows = padded_prompt_entries.shape[0] // requests
    per_group_view, embedding_dimension = present_reward.shape
    seq_count = lax.axis_size("z") * lax.axis_size("core")
    arrived = seq_shift(continued_prompt_entries[-1:], 1, seq_count)
    first = seq_index() == 0
    edge_row = jnp.where(first, preceding_entry_line[None, :], arrived)
    stacked = jnp.concatenate([continued_prompt_entries, padded_prompt_entries, edge_row], axis=0)
    stacked = lax.all_gather(stacked, "mp", axis=1, tiled=True)
    current = stacked[: long_rows + padded_prompt_entries.shape[0]]
    edge_full = stacked[-1:]
    previous = shifted_rows(current, edge_full, long_rows, requests, slot_rows)
    mixes = [mix_rows(current, previous, token_mixing_ratios[index]) for index in range(5)]
    total_rows = current.shape[0]
    columns = acceptance_transform.shape[1]
    blocks = jnp.stack(
        [
            acceptance_transform,
            lookup_transform,
            payload_transform,
            gating_transform,
            final_transform.T,
        ],
        axis=0,
    )
    blocks = lax.all_gather(lax.all_gather(blocks, "z"), "core")
    cores, chips, kinds, depth, width = blocks.shape
    blocks = jnp.transpose(blocks, (2, 1, 0, 3, 4)).reshape(kinds, chips * cores * depth, width)
    pieces = tuple((blocks[index] for index in range(4)))
    acceptance_entries, lookup_entries, payload_entries, gate = tuple(
        (
            jnp.dot(source, piece, preferred_element_type=jnp.float32)
            for source, piece in zip(mixes[:4], pieces)
        )
    )
    squeezed = jnp.tanh(
        jnp.dot(mixes[4], fading_left_factor, preferred_element_type=jnp.float32)
    ).astype(jnp.bfloat16)
    log_fading_amount = -jnp.exp(
        fading_baseline[None, :]
        + jnp.dot(squeezed, fading_right_factor, preferred_element_type=jnp.float32)
    )
    recept3, keys3, values3, decay3 = [
        a.reshape(total_rows, per_group_view, embedding_dimension)
        for a in (acceptance_entries, lookup_entries, payload_entries, log_fading_amount)
    ]
    local_state, long_out = continued_recurrence(
        recept3[:long_rows],
        keys3[:long_rows],
        values3[:long_rows],
        decay3[:long_rows],
        present_reward,
    )
    long_decay = decay3[:long_rows]
    group_total = jnp.sum(long_decay, axis=0)
    start = (jnp.zeros((per_group_view, embedding_dimension), jnp.float32), carried_memory)
    _, incoming = exclusive_prefix((group_total, local_state), start, seq_count)
    before_row = jnp.cumsum(long_decay, axis=0) - long_decay
    long_out = long_out + jnp.einsum(
        "ihc,hcd->ihd", recept3[:long_rows] * jnp.exp(before_row), incoming, precision=highest
    )
    span_end = jnp.exp(group_total)[:, :, None] * incoming + local_state
    live_rows = (
        lax.broadcasted_iota(jnp.int32, (requests, slot_rows), 1) < prompt_live_extents[:, None]
    )
    live_flat = live_rows.reshape(requests * slot_rows).astype(jnp.float32)[:, None, None]
    short_shape = (requests, slot_rows, per_group_view, embedding_dimension)
    short_recept = recept3[long_rows:].reshape(short_shape)
    short_keys = (keys3[long_rows:] * live_flat).reshape(short_shape)
    short_values = values3[long_rows:].reshape(short_shape)
    short_decay = (decay3[long_rows:] * live_flat).reshape(short_shape)
    zeroed_memory = jnp.zeros(
        (per_group_view, embedding_dimension, embedding_dimension), jnp.float32
    )

    def request_pass(acceptance_lines, lookup_table, payload_table, fading_table):
        return block_sweep(
            zeroed_memory,
            acceptance_lines,
            lookup_table,
            payload_table,
            fading_table,
            present_reward,
        )

    request_states, short_out = jax.vmap(request_pass)(
        short_recept, short_keys, short_values, short_decay
    )
    wkv = jnp.concatenate(
        [long_out, short_out.reshape(requests * slot_rows, per_group_view, embedding_dimension)],
        axis=0,
    )
    mean = jnp.mean(wkv, axis=-1, keepdims=True)
    centred = wkv - mean
    variance = jnp.mean(centred * centred, axis=-1, keepdims=True)
    normed = (centred * lax.rsqrt(variance + norm_eps)).reshape(
        total_rows, columns
    ) * group_layer_scaling[None, :] + group_layer_shift_term[None, :]
    row_live = jnp.concatenate(
        [jnp.ones((long_rows,), dtype=bool), live_rows.reshape(requests * slot_rows)], axis=0
    )
    hidden = jnp.where(row_live[:, None], normed * jax.nn.silu(gate), 0.0).astype(jnp.bfloat16)
    full_out = blocks[4]
    mixed_rows = lax.psum_scatter(
        lax.dot_general(
            hidden, full_out, (((1,), (1,)), ((), ())), preferred_element_type=jnp.float32
        ),
        "mp",
        scatter_dimension=0,
        tiled=True,
    )
    return (mixed_rows.astype(jnp.bfloat16)[None], span_end[None], request_states)


def solution(mesh):
    placed = (
        P("seq", "mp"),
        P("seq", "mp"),
        P("seq"),
        P("mp"),
        P("mp", None, None),
        P(),
        P("seq", "mp"),
        P("seq", "mp"),
        P("seq", "mp"),
        P("seq", "mp"),
        P("mp"),
        P(),
        P(None, "mp"),
        P("mp", None),
        P("mp"),
        P("mp"),
        P("mp", "seq"),
    )
    devices = mesh.devices
    seq_devices, mp_devices = devices.shape
    mesh = jax.sharding.Mesh(devices.reshape(seq_devices // 2, 2, mp_devices), ("z", "core", "mp"))
    placed = tuple((P(*[SEQ if name == "seq" else name for name in spec]) for spec in placed))
    return jax.shard_map(
        on_device,
        mesh=mesh,
        in_specs=placed,
        out_specs=(P(SEQ, "mp", None), P(SEQ, "mp", None, None), P(SEQ, "mp", None, None)),
        check_vma=False,
    )
```

profile of v0, /device:TPU:2, one launch (start us, length us, event | category | flops | bytes accessed | tf_op | source)
XLA Modules:
  0.0 407.3 jit_solution(4726152788664702614)
XLA Ops:
  17.9 80.3 %all-gather.8.cloned.1.call-done = bf16[80,128,256]{2,1,0:T(8,128)(2,1)} async-done(((bf16[5,128,256]{2,1,0:T(8,128)(2,1)}), bf16[80,128,256]{2,1,0:T(8,128)(2,1)}) %all-gather.8.cloned.1.call-update) | async-done | bytes 5242896 | tf_op jit(solution)/shard_map/all_gather | solution.py:164
  99.8 60.9 %all-gather.6.cloned.1.call-done = bf16[257,4096]{1,0:T(8,128)(2,1)} async-done(((bf16[257,256]{1,0:T(8,128)(2,1)}), bf16[257,4096]{1,0:T(8,128)(2,1)}) %all-gather.6.cloned.1.call-update) | async-done | bytes 2105360 | tf_op jit(solution)/shard_map/all_gather | solution.py:147
  160.7 1.9 slice-done
  164.0 3.0 fusion.40
  169.3 4.1 %collective-permute-start.2 = (f32[4,64]{1,0:T(4,128)S(1)}, f32[4,64]{1,0:T(4,128)S(1)}, u32[]{:S(2)}, u32[]{:S(2)}) collective-permute-start(f32[4,64]{1,0:T(4,128)S(1)} %get-tuple-element.130), channel_id=1, source_target_pairs={{0,16},{16,32},{32,48},{48,64},{64,80},{80,96},{96,112},{112,128},... | collective-permute-start | bytes 3080 | tf_op jit(solution)/shard_map/ppermute | solution.py:18
  174.4 6.0 %collective-permute-start.3 = (f32[4,64]{1,0:T(4,128)S(1)}, f32[4,64]{1,0:T(4,128)S(1)}, u32[]{:S(2)}, u32[]{:S(2)}) collective-permute-start(f32[4,64]{1,0:T(4,128)S(1)} %get-tuple-element.128), channel_id=1, source_target_pairs={{0,32},{16,48},{32,64},{48,80},{64,96},{80,112},{96,128},{112,144}... | collective-permute-start | bytes 3080 | tf_op jit(solution)/shard_map/ppermute | solution.py:18
  181.8 5.2 %collective-permute-start.4 = (f32[4,64]{1,0:T(4,128)S(1)}, f32[4,64]{1,0:T(4,128)S(1)}, u32[]{:S(2)}, u32[]{:S(2)}) collective-permute-start(f32[4,64]{1,0:T(4,128)S(1)} %get-tuple-element.126), channel_id=1, source_target_pairs={{0,64},{16,80},{32,96},{48,112},{64,128},{80,144},{96,160},{112,17... | collective-permute-start | bytes 3080 | tf_op jit(solution)/shard_map/ppermute | solution.py:18
  188.2 13.1 %collective-permute-start.5 = (f32[4,64]{1,0:T(4,128)S(1)}, f32[4,64]{1,0:T(4,128)S(1)}, u32[]{:S(2)}, u32[]{:S(2)}) collective-permute-start(f32[4,64]{1,0:T(4,128)S(1)} %get-tuple-element.124), channel_id=1, source_target_pairs={{0,128},{16,144},{32,160},{48,176},{64,192},{80,208},{96,224},{112... | collective-permute-start | bytes 3080 | tf_op jit(solution)/shard_map/ppermute | solution.py:18
  201.4 6.2 %fusion.92 = (bf16[1,16,2,128,256]{4,3,0,1,2:T(8,128)(2,1)}, bf16[1,16,2,128,256]{4,3,0,1,2:T(8,128)(2,1)}, bf16[1,16,2,128,256]{4,3,0,1,2:T(8,128)(2,1)S(1)}, b...) fusion(bf16[5,16,2,128,256]{4,3,0,1,2:T(8,128)(2,1)} %bitcast.142), kind=kLoop, calls=%fused_computation.139 | loop fusion | bytes 20971520 | tf_op jit(solution)/shard_map/slice | solution.py:167
  217.1 13.2 %while.13 = (s32[]{:T(128)}, f32[4,64,64]{2,1,0:T(8,128)S(1)}, f32[2,64,4,64]{1,0,3,2:T(2,128)}, f32[2,64,4,64]{1,0,3,2:T(2,128)S(1)}, f32[2,64,4,64]{3,2,1,0:T(...) while((s32[]{:T(128)}, f32[4,64,64]{2,1,0:T(8,128)S(1)}, ...), condition=%wide.region_3.4_spmd.clone, body=%wide.region_0.3_spmd.clone.sunk | while | flops 51646208 | bytes 2444424 | solution.py:96
  219.4 4.3 %dynamic_update_slice.6 = f32[2,64,4,64]{1,0,3,2:T(2,128)} dynamic-update-slice(f32[2,64,4,64]{1,0,3,2:T(2,128)} %get-tuple-element.235, f32[1,64,4,64]{1,0,3,2:T(1,128)S(1)} %copy.218, s32[]{:T(128)S(6)} %copy.227, s32[]{:T(128)} %constant.28.clone.1..sunk, s32[]{:T(128)} %constant.28.clone.1..sunk, s32[]{:T(128)} %constant.28.clone.1..sunk) | dynamic-update-slice | bytes 131076 | tf_op jit(solution)/shard_map/while/body/jit(dynamic_update_index_in_dim)/dynamic_update_slice | solution.py:96
  226.1 4.3 %dynamic_update_slice.6 = f32[2,64,4,64]{1,0,3,2:T(2,128)} dynamic-update-slice(f32[2,64,4,64]{1,0,3,2:T(2,128)} %get-tuple-element.235, f32[1,64,4,64]{1,0,3,2:T(1,128)S(1)} %copy.218, s32[]{:T(128)S(6)} %copy.227, s32[]{:T(128)} %constant.28.clone.1..sunk, s32[]{:T(128)} %constant.28.clone.1..sunk, s32[]{:T(128)} %constant.28.clone.1..sunk) | dynamic-update-slice | bytes 131076 | tf_op jit(solution)/shard_map/while/body/jit(dynamic_update_index_in_dim)/dynamic_update_slice | solution.py:96
  236.5 2.1 exponential_multiply_fusion
  238.6 5.3 %collective-permute-start.8 = (f32[4,64,64]{2,1,0:T(8,128)S(1)}, f32[4,64,64]{2,1,0:T(8,128)S(1)}, u32[]{:S(2)}, u32[]{:S(2)}) collective-permute-start(f32[4,64,64]{2,1,0:T(8,128)S(1)} %add_select_fusion.4), channel_id=1, source_target_pairs={{0,32},{16,48},{32,64},{48,80},{64,96},{80,112},{96,128},{112,144}... | collective-permute-start | bytes 196616 | tf_op jit(solution)/shard_map/ppermute | solution.py:18
  244.9 2.5 collective-permute-done.8
  247.5 6.3 %collective-permute-start.9 = (f32[4,64,64]{2,1,0:T(8,128)S(1)}, f32[4,64,64]{2,1,0:T(8,128)S(1)}, u32[]{:S(2)}, u32[]{:S(2)}) collective-permute-start(f32[4,64,64]{2,1,0:T(8,128)S(1)} %add_select_fusion.3), channel_id=1, source_target_pairs={{0,64},{16,80},{32,96},{48,112},{64,128},{80,144},{96,160},{112,17... | collective-permute-start | bytes 196616 | tf_op jit(solution)/shard_map/ppermute | solution.py:18
  254.4 3.2 collective-permute-done.9
  257.7 12.6 %collective-permute-start.10 = (f32[4,64,64]{2,1,0:T(8,128)S(1)}, f32[4,64,64]{2,1,0:T(8,128)S(1)}, u32[]{:S(2)}, u32[]{:S(2)}) collective-permute-start(f32[4,64,64]{2,1,0:T(8,128)S(1)} %add_select_fusion.2), channel_id=1, source_target_pairs={{0,128},{16,144},{32,160},{48,176},{64,192},{80,208},{96,224},{112... | collective-permute-start | bytes 196616 | tf_op jit(solution)/shard_map/ppermute | solution.py:18
  273.0 13.9 %collective-permute-start.11 = (f32[4,64,64]{2,1,0:T(8,128)S(1)}, f32[4,64,64]{2,1,0:T(8,128)}, u32[]{:S(2)}, u32[]{:S(2)}) collective-permute-start(f32[4,64,64]{2,1,0:T(8,128)S(1)} %add_select_fusion.1), channel_id=1, source_target_pairs={{0,256},{16,272},{32,288},{48,304},{64,320},{80,336},{96,352},{112... | collective-permute-start | bytes 196616 | tf_op jit(solution)/shard_map/ppermute | solution.py:18
  289.5 3.3 copy.156
  296.4 1.8 concatenate.27
  302.4 1.8 copy.154
  307.5 7.5 %fusion.68 = f32[256,4096]{1,0:T(8,128)} fusion(bf16[4096,256]{1,0:T(8,128)(2,1)} %bitcast.145, f32[256,256]{1,0:T(8,128)} %copy.154, f32[256,256]{1,0:T(8,128)} %copy.153, f32[128,256]{1,0:T(8,128)} %concatenate.27, f32[128,256]{1,0:T(8,128)} %copy.151, bf16[4096,256]{1,0:T(8,128)(2,1)} %bitcast.146, f32[4096]{0:T(1024)S(1)} %bitcast.160, ...), kind=kOutput, calls=%fused_computation.84 | convolution fusion | flops 1086062592 | bytes 13396480 | tf_op jit(solution)/shard_map/dot_general | solution.py:243
  319.0 80.1 %reduce-scatter.2.cloned.1.call-done = f32[16,4096]{1,0:T(8,128)} async-done(((f32[256,4096]{1,0:T(8,128)}), f32[16,4096]{1,0:T(8,128)}) %reduce-scatter.2.cloned.1.call-update) | async-done | bytes 262160 | tf_op jit(solution)/shard_map/reduce_scatter | solution.py:242
  (199 shorter events, 62.9 us)
Async XLA Ops:
  7.2 156.8 %copy-start = (bf16[4096,128]{1,0:T(8,128)(2,1)S(1)}, bf16[4096,128]{1,0:T(8,128)(2,1)}, u32[]{:S(2)}) copy-start(bf16[4096,128]{1,0:T(8,128)(2,1)} %param.30) | copy-start | bytes 3145732
  7.2 91.1 %all-gather.8.cloned.1.call-start = ((), (), s32[]{:S(2)}) async-start(), calls=%async_computation.3 | async-start | bytes 5570560 | tf_op jit(solution)/shard_map/all_gather | solution.py:164
  12.4 148.3 %all-gather.6.cloned.1.call-start = ((), (), s32[]{:S(2)}) async-start(), calls=%async_computation.1 | async-start | bytes 2297856 | tf_op jit(solution)/shard_map/all_gather | solution.py:147
  13.1 2.5 collective-permute-start
  17.9 183.5 %all-gather.10.cloned.1.call-start = ((), (), s32[]{:S(2)}) async-start(), calls=%async_computation.4 | async-start | bytes 15728640 | tf_op jit(solution)/shard_map/all_gather | solution.py:164
  98.3 300.9 %reduce-scatter.2.cloned.1.call-start = ((), (), s32[]{:S(2)}) async-start(), calls=%async_computation.2 | async-start | bytes 4456448 | tf_op jit(solution)/shard_map/reduce_scatter | solution.py:242
  167.2 2.1 collective-permute-start.1
  169.3 5.1 %collective-permute-start.2 = (f32[4,64]{1,0:T(4,128)S(1)}, f32[4,64]{1,0:T(4,128)S(1)}, u32[]{:S(2)}, u32[]{:S(2)}) collective-permute-start(f32[4,64]{1,0:T(4,128)S(1)} %get-tuple-element.130), channel_id=1, source_target_pairs={{0,16},{16,32},{32,48},{48,64},{64,80},{80,96},{96,112},{112,128},... | collective-permute-start | bytes 3080 | tf_op jit(solution)/shard_map/ppermute | solution.py:18
  174.4 33.2 %copy-start.7 = (f32[2,64,4,64]{3,2,1,0:T(4,128)}, f32[2,64,4,64]{3,2,1,0:T(4,128)S(1)}, u32[]{:S(2)}) copy-start(f32[2,64,4,64]{3,2,1,0:T(4,128)S(1)} %copy.141) | copy-start | bytes 393220
  174.4 7.3 %collective-permute-start.3 = (f32[4,64]{1,0:T(4,128)S(1)}, f32[4,64]{1,0:T(4,128)S(1)}, u32[]{:S(2)}, u32[]{:S(2)}) collective-permute-start(f32[4,64]{1,0:T(4,128)S(1)} %get-tuple-element.128), channel_id=1, source_target_pairs={{0,32},{16,48},{32,64},{48,80},{64,96},{80,112},{96,128},{112,144}... | collective-permute-start | bytes 3080 | tf_op jit(solution)/shard_map/ppermute | solution.py:18
  181.8 6.5 %collective-permute-start.4 = (f32[4,64]{1,0:T(4,128)S(1)}, f32[4,64]{1,0:T(4,128)S(1)}, u32[]{:S(2)}, u32[]{:S(2)}) collective-permute-start(f32[4,64]{1,0:T(4,128)S(1)} %get-tuple-element.126), channel_id=1, source_target_pairs={{0,64},{16,80},{32,96},{48,112},{64,128},{80,144},{96,160},{112,17... | collective-permute-start | bytes 3080 | tf_op jit(solution)/shard_map/ppermute | solution.py:18
  188.2 43.4 %collective-permute-start.5 = (f32[4,64]{1,0:T(4,128)S(1)}, f32[4,64]{1,0:T(4,128)S(1)}, u32[]{:S(2)}, u32[]{:S(2)}) collective-permute-start(f32[4,64]{1,0:T(4,128)S(1)} %get-tuple-element.124), channel_id=1, source_target_pairs={{0,128},{16,144},{32,160},{48,176},{64,192},{80,208},{96,224},{112... | collective-permute-start | bytes 3080 | tf_op jit(solution)/shard_map/ppermute | solution.py:18
  230.3 3.7 collective-permute-start.6
  232.7 11.8 %copy-start.19 = (f32[128,256]{1,0:T(8,128)S(1)}, f32[128,256]{1,0:T(8,128)}, u32[]{:S(2)}) copy-start(f32[128,256]{1,0:T(8,128)} %get-tuple-element.152) | copy-start | bytes 393220
  235.0 3.5 collective-permute-start.7
  238.6 8.7 %collective-permute-start.8 = (f32[4,64,64]{2,1,0:T(8,128)S(1)}, f32[4,64,64]{2,1,0:T(8,128)S(1)}, u32[]{:S(2)}, u32[]{:S(2)}) collective-permute-start(f32[4,64,64]{2,1,0:T(8,128)S(1)} %add_select_fusion.4), channel_id=1, source_target_pairs={{0,32},{16,48},{32,64},{48,80},{64,96},{80,112},{96,128},{112,144}... | collective-permute-start | bytes 196616 | tf_op jit(solution)/shard_map/ppermute | solution.py:18
  244.8 43.8 %copy-start.5 = (f32[2,64,4,64]{1,3,2,0:T(8,128)}, f32[2,64,4,64]{1,3,2,0:T(8,128)S(1)}, u32[]{:S(2)}) copy-start(f32[2,64,4,64]{1,3,2,0:T(8,128)S(1)} %copy.145) | copy-start | bytes 393220
  247.5 10.1 %collective-permute-start.9 = (f32[4,64,64]{2,1,0:T(8,128)S(1)}, f32[4,64,64]{2,1,0:T(8,128)S(1)}, u32[]{:S(2)}, u32[]{:S(2)}) collective-permute-start(f32[4,64,64]{2,1,0:T(8,128)S(1)} %add_select_fusion.3), channel_id=1, source_target_pairs={{0,64},{16,80},{32,96},{48,112},{64,128},{80,144},{96,160},{112,17... | collective-permute-start | bytes 196616 | tf_op jit(solution)/shard_map/ppermute | solution.py:18
  257.7 15.1 %collective-permute-start.10 = (f32[4,64,64]{2,1,0:T(8,128)S(1)}, f32[4,64,64]{2,1,0:T(8,128)S(1)}, u32[]{:S(2)}, u32[]{:S(2)}) collective-permute-start(f32[4,64,64]{2,1,0:T(8,128)S(1)} %add_select_fusion.2), channel_id=1, source_target_pairs={{0,128},{16,144},{32,160},{48,176},{64,192},{80,208},{96,224},{112... | collective-permute-start | bytes 196616 | tf_op jit(solution)/shard_map/ppermute | solution.py:18
  273.0 19.8 %copy-start.9 = (f32[4,64,64]{2,1,0:T(8,128)}, f32[4,64,64]{2,1,0:T(8,128)S(1)}, u32[]{:S(2)}) copy-start(f32[4,64,64]{2,1,0:T(8,128)S(1)} %add_select_fusion.1) | copy-start | bytes 196612
  273.0 26.8 %collective-permute-start.11 = (f32[4,64,64]{2,1,0:T(8,128)S(1)}, f32[4,64,64]{2,1,0:T(8,128)}, u32[]{:S(2)}, u32[]{:S(2)}) collective-permute-start(f32[4,64,64]{2,1,0:T(8,128)S(1)} %add_select_fusion.1), channel_id=1, source_target_pairs={{0,256},{16,272},{32,288},{48,304},{64,320},{80,336},{96,352},{112... | collective-permute-start | bytes 196616 | tf_op jit(solution)/shard_map/ppermute | solution.py:18
  289.5 8.7 %copy-start.1 = (bf16[1,16,2,128,256]{4,3,0,1,2:T(8,128)(2,1)S(1)}, bf16[1,16,2,128,256]{4,3,0,1,2:T(8,128)(2,1)}, u32[]{:S(2)}) copy-start(bf16[1,16,2,128,256]{4,3,0,1,2:T(8,128)(2,1)} %get-tuple-element.137) | copy-start | bytes 6291460
  299.7 7.7 %copy-start.31 = (f32[256]{0:T(256)S(1)}, f32[256]{0:T(256)}, u32[]{:S(2)}) copy-start(f32[256]{0:T(256)} %param.33) | copy-start | bytes 3076
  299.7 7.7 %copy-start.32 = (pred[256]{0:T(512)(128)(4,1)S(1)}, pred[256]{0:T(512)(128)(4,1)}, u32[]{:S(2)}) copy-start(pred[256]{0:T(512)(128)(4,1)} %concatenate.22) | copy-start | bytes 772
  (26 other events, 71.3 us)
Sparse Core Ops, SparseCore 0:
  12.5 85.6 all-gather.7
  101.8 58.8 all-gather.5
  162.8 33.1 all-gather.9
  315.1 83.9 reduce-scatter.1
where the time goes:
time: 409 us; the launch traced here: 407 us
  waiting for transfers between devices  232 us (57%)
  starting transfers between devices  72.5 us (18%)
  local copies, waits for them, and re-layouts  54.7 us (13%)
  matrix products  21.7 us (5%)
  between operations  14.5 us (4%)
  other arithmetic  11.6 us (3%)
    all_gather x2, waiting for transfers between devices, on_device(): blocks = lax.all_gather(lax.all_gather(blocks, 'z'), 'core')  80.3 us
    reduce_scatter x1, waiting for transfers between devices, on_device(): lax.psum_scatter(lax.dot_general(hidden, full_out, (((1,), (1,)), ((), ()...  80.1 us
    ppermute x12, starting transfers between devices, seq_shift(): return lax.ppermute(x, SEQ, pairs)  72.3 us
    all_gather x1, waiting for transfers between devices, on_device(): stacked = lax.all_gather(stacked, 'mp', axis=1, tiled=True)  60.9 us
    ppermute x12, waiting for transfers between devices, seq_shift(): return lax.ppermute(x, SEQ, pairs)  10.7 us
    unnamed x71, local copies, waits for them, and re-layouts  10.1 us
    dynamic_update_slice x4, local copies, waits for them, and re-layouts, continued_recurrence(): lax.scan(step, jnp.zeros((per_group_view, embedding_dimension, embedding_...  8.76 us
  transfers between devices with their start and end apart: 16, of which 10 were waited for; matrix products, arithmetic and copies ran while one was open for 14% of the time, Pallas kernels for 0%

commit v1 on v0

--- a/solution.py
+++ b/solution.py
@@ -144,7 +144,9 @@
     first = seq_index() == 0
     edge_row = jnp.where(first, preceding_entry_line[None, :], arrived)
     stacked = jnp.concatenate([continued_prompt_entries, padded_prompt_entries, edge_row], axis=0)
-    stacked = lax.all_gather(stacked, "mp", axis=1, tiled=True)
+    stacked = jnp.concatenate(
+        lax.all_to_all(jnp.stack([stacked] * lax.axis_size("mp")), "mp", 0, 0), axis=1
+    )
     current = stacked[: long_rows + padded_prompt_entries.shape[0]]
     edge_full = stacked[-1:]
     previous = shifted_rows(current, edge_full, long_rows, requests, slot_rows)

time: 409 us -> 418 us (1.022)
  waiting for transfers between devices: 232 us -> 202 us
  local copies, waits for them, and re-layouts: 54.7 us -> 78 us
  other arithmetic: 11.6 us -> 33 us
    all_gather x1 -> x0, waiting for transfers between devices: 60.9 us -> none  [on_device(): stacked = lax.all_gather(stacked, 'mp', axis=1, tiled=True)]
    all_to_all x0 -> x1, waiting for transfers between devices: none -> 26 us  [on_device(): lax.all_to_all(jnp.stack([stacked] * lax.axis_size('mp')), 'mp', 0, 0)]
    convert_element_type x0 -> x3, other arithmetic: none -> 15.6 us  [mix_rows(): (here + weight[None, :] * (previous.astype(jnp.float32) - here)).astype(j...]
    ppermute x12, starting transfers between devices: 72.3 us -> 61.2 us  [seq_shift(): return lax.ppermute(x, SEQ, pairs)]
    all_to_all x0 -> x1, starting transfers between devices: none -> 7.24 us  [on_device(): lax.all_to_all(jnp.stack([stacked] * lax.axis_size('mp')), 'mp', 0, 0)]
    all_gather x2, waiting for transfers between devices: 80.3 us -> 85.8 us  [on_device(): blocks = lax.all_gather(lax.all_gather(blocks, 'z'), 'core')]
    ppermute x12, waiting for transfers between devices: 10.7 us -> 5.85 us  [seq_shift(): return lax.ppermute(x, SEQ, pairs)]
    reshape x0 -> x2, local copies, waits for them, and re-layouts: none -> 4.6 us  [the longest x1 2.32 us: shifted_rows(): short_view = current[long_rows:].reshape(requests, slot_rows, feature_part)]
  transfers between devices with their start and end apart: 16 -> 16, of which waited for: 10 -> 7; matrix products, arithmetic and copies ran while one was open for 14% -> 25% of each run, Pallas kernels for 0% -> 0%
where the time goes in v1:
time: 418 us; the launch traced here: 416 us
  waiting for transfers between devices  202 us (48%)
  local copies, waits for them, and re-layouts  78 us (19%)
  starting transfers between devices  68.5 us (16%)
  other arithmetic  33 us (8%)
  matrix products  19.2 us (5%)
  between operations  14.4 us (3%)
    all_gather x2, waiting for transfers between devices, on_device(): blocks = lax.all_gather(lax.all_gather(blocks, 'z'), 'core')  85.8 us
    reduce_scatter x1, waiting for transfers between devices, on_device(): lax.psum_scatter(lax.dot_general(hidden, full_out, (((1,), (1,)), ((), ()...  84.5 us
    ppermute x12, starting transfers between devices, seq_shift(): return lax.ppermute(x, SEQ, pairs)  61.2 us
    all_to_all x1, waiting for transfers between devices, on_device(): lax.all_to_all(jnp.stack([stacked] * lax.axis_size('mp')), 'mp', 0, 0)  26 us
    convert_element_type x3, other arithmetic, mix_rows(): (here + weight[None, :] * (previous.astype(jnp.float32) - here)).astype(j...  15.6 us
    unnamed x72, local copies, waits for them, and re-layouts  13.1 us
    dynamic_update_slice x4, local copies, waits for them, and re-layouts, continued_recurrence(): lax.scan(step, jnp.zeros((per_group_view, embedding_dimension, embedding_...  8.77 us
  transfers between devices with their start and end apart: 16, of which 7 were waited for; matrix products, arithmetic and copies ran while one was open for 25% of the time, Pallas kernels for 0%

profile of v1, /device:TPU:2, one launch (start us, length us, event | category | flops | bytes accessed | tf_op | source)
XLA Modules:
  0.0 415.5 jit_solution(3519379236690200677)
XLA Ops:
  12.4 85.8 %all-gather.5.cloned.1.call-done = bf16[80,128,256]{2,1,0:T(8,128)(2,1)} async-done(((bf16[5,128,256]{2,1,0:T(8,128)(2,1)}), bf16[80,128,256]{2,1,0:T(8,128)(2,1)}) %all-gather.5.cloned.1.call-update) | async-done | bytes 5242896 | tf_op jit(solution)/shard_map/all_gather | solution.py:166
  102.7 7.2 %all-to-all-start = ((bf16[16,257,256]{2,1,0:T(8,128)(2,1)}), bf16[16,257,256]{2,1,0:T(8,128)(2,1)S(1)}, u32[]{:S(2)}, u32[]{:S(2)}) async-start(bf16[16,257,256]{2,1,0:T(8,128)(2,1)} %stack.14), calls=%async_computation | async-start | bytes 4325376 | tf_op jit(solution)/shard_map/all_to_all | solution.py:148
  114.5 26.0 %all-to-all-done = bf16[16,257,256]{2,1,0:T(8,128)(2,1)S(1)} async-done(((bf16[16,257,256]{2,1,0:T(8,128)(2,1)}), bf16[16,257,256]{2,1,0:T(8,128)(2,1)S(1)}, u32[]{:S(2)}, u32[]{:S(2)}) %all-to-all-start) | async-done | bytes 2105376 | tf_op jit(solution)/shard_map/all_to_all | solution.py:148
  140.5 2.8 copy.136
  148.2 2.7 copy.137
  161.8 4.6 %fusion.22 = bf16[256,4096]{0,1:T(8,128)(2,1)} fusion(bf16[128,4096]{0,1:T(8,128)(2,1)} %copy.138, bf16[127,4096]{0,1:T(8,128)(2,1)S(1)} %bitcast.167, bf16[1,4096]{0,1:T(8,128)(2,1)S(1)} %bitcast.168, f32[4096]{0:T(1024)S(1)} %bitcast.189, bf16[257,16,256]{0,2,1:T(8,128)(2,1)} %bitcast.164), kind=kLoop, calls=%fused_computation.44 | loop fusion | flops 11534336 | bytes 6307840 | tf_op jit(solution)/shard_map/convert_element_type | solution.py:36
  169.8 2.9 collective-permute-start.1
  172.7 7.6 %fusion.20 = (bf16[256,16,256]{0,2,1:T(8,128)(2,1)}, bf16[256,16,256]{0,2,1:T(8,128)(2,1)}, bf16[256,16,256]{0,2,1:T(8,128)(2,1)}) fusion(f32[16,256]{1,0:T(8,128)} %mul.267, bf16[257,16,256]{0,2,1:T(8,128)(2,1)} %bitcast.165, bf16[128,16,256]{0,2,1:T(8,128)(2,1)} %copy.139, bf16[127,16,256]{0,2,1:T(8,128)(2,1)S(1)} %slice.146, ...), kind=kLoop, calls=%fused_computation.40 | loop fusion | flops 17825792 | bytes 10534912 | tf_op jit(solution)/shard_map/convert_element_type | solution.py:36
  183.0 3.4 fusion.17
  186.8 3.0 collective-permute-start.3
  191.1 4.5 %collective-permute-start.4 = (f32[4,64]{1,0:T(4,128)S(1)}, f32[4,64]{1,0:T(4,128)S(1)}, u32[]{:S(2)}, u32[]{:S(2)}) collective-permute-start(f32[4,64]{1,0:T(4,128)S(1)} %get-tuple-element.130), channel_id=1, source_target_pairs={{0,64},{16,80},{32,96},{48,112},{64,128},{80,144},{96,160},{112,17... | collective-permute-start | bytes 3080 | tf_op jit(solution)/shard_map/ppermute | solution.py:18
  198.5 7.3 %collective-permute-start.5 = (f32[4,64]{1,0:T(4,128)S(1)}, f32[4,64]{1,0:T(4,128)S(1)}, u32[]{:S(2)}, u32[]{:S(2)}) collective-permute-start(f32[4,64]{1,0:T(4,128)S(1)} %get-tuple-element.128), channel_id=1, source_target_pairs={{0,128},{16,144},{32,160},{48,176},{64,192},{80,208},{96,224},{112... | collective-permute-start | bytes 3080 | tf_op jit(solution)/shard_map/ppermute | solution.py:18
  205.8 5.8 %fusion.62 = (bf16[1,16,2,128,256]{4,3,0,1,2:T(8,128)(2,1)S(1)}, bf16[1,16,2,128,256]{4,3,0,1,2:T(8,128)(2,1)}, bf16[1,16,2,128,256]{4,3,0,1,2:T(8,128)(2,1)S(1)...) fusion(bf16[5,16,2,128,256]{4,3,0,1,2:T(8,128)(2,1)} %bitcast.169), kind=kLoop, calls=%fused_computation.130 | loop fusion | bytes 20971520 | tf_op jit(solution)/shard_map/slice | solution.py:169
  223.5 18.7 %while.13 = (s32[]{:T(128)}, f32[4,64,64]{2,1,0:T(8,128)S(1)}, f32[2,64,4,64]{1,0,3,2:T(2,128)}, f32[2,64,4,64]{1,0,3,2:T(2,128)S(1)}, f32[2,64,4,64]{3,2,1,0:T(...) while((s32[]{:T(128)}, f32[4,64,64]{2,1,0:T(8,128)S(1)}, ...), condition=%wide.region_3.4_spmd.clone, body=%wide.region_0.3_spmd.clone.sunk | while | flops 51646208 | bytes 2444424 | solution.py:96
  228.6 4.3 %dynamic_update_slice.6 = f32[2,64,4,64]{1,0,3,2:T(2,128)} dynamic-update-slice(f32[2,64,4,64]{1,0,3,2:T(2,128)} %get-tuple-element.238, f32[1,64,4,64]{1,0,3,2:T(1,128)S(1)} %copy.231, s32[]{:T(128)S(6)} %copy.240, s32[]{:T(128)} %constant.28.clone.1..sunk, s32[]{:T(128)} %constant.28.clone.1..sunk, s32[]{:T(128)} %constant.28.clone.1..sunk) | dynamic-update-slice | bytes 131076 | tf_op jit(solution)/shard_map/while/body/jit(dynamic_update_index_in_dim)/dynamic_update_slice | solution.py:96
  238.0 4.3 %dynamic_update_slice.6 = f32[2,64,4,64]{1,0,3,2:T(2,128)} dynamic-update-slice(f32[2,64,4,64]{1,0,3,2:T(2,128)} %get-tuple-element.238, f32[1,64,4,64]{1,0,3,2:T(1,128)S(1)} %copy.231, s32[]{:T(128)S(6)} %copy.240, s32[]{:T(128)} %constant.28.clone.1..sunk, s32[]{:T(128)} %constant.28.clone.1..sunk, s32[]{:T(128)} %constant.28.clone.1..sunk) | dynamic-update-slice | bytes 131076 | tf_op jit(solution)/shard_map/while/body/jit(dynamic_update_index_in_dim)/dynamic_update_slice | solution.py:96
  251.9 6.7 %collective-permute-start.8 = (f32[4,64,64]{2,1,0:T(8,128)}, f32[4,64,64]{2,1,0:T(8,128)}, u32[]{:S(2)}, u32[]{:S(2)}) collective-permute-start(f32[4,64,64]{2,1,0:T(8,128)} %add_select_fusion.4), channel_id=1, source_target_pairs={{0,32},{16,48},{32,64},{48,80},{64,96},{80,112},{96,128},{112,144}... | collective-permute-start | bytes 196616 | tf_op jit(solution)/shard_map/ppermute | solution.py:18
  263.3 3.4 collective-permute-start.9
  267.2 2.8 collective-permute-done.9
  270.8 12.7 %collective-permute-start.10 = (f32[4,64,64]{2,1,0:T(8,128)}, f32[4,64,64]{2,1,0:T(8,128)}, u32[]{:S(2)}, u32[]{:S(2)}) collective-permute-start(f32[4,64,64]{2,1,0:T(8,128)} %add_select_fusion.2), channel_id=1, source_target_pairs={{0,128},{16,144},{32,160},{48,176},{64,192},{80,208},{96,224},{112... | collective-permute-start | bytes 196616 | tf_op jit(solution)/shard_map/ppermute | solution.py:18
  286.7 13.9 %collective-permute-start.11 = (f32[4,64,64]{2,1,0:T(8,128)S(1)}, f32[4,64,64]{2,1,0:T(8,128)}, u32[]{:S(2)}, u32[]{:S(2)}) collective-permute-start(f32[4,64,64]{2,1,0:T(8,128)S(1)} %add_select_fusion.1), channel_id=1, source_target_pairs={{0,256},{16,272},{32,288},{48,304},{64,320},{80,336},{96,352},{112... | collective-permute-start | bytes 196616 | tf_op jit(solution)/shard_map/ppermute | solution.py:18
  302.5 3.2 copy.168
  311.8 6.6 %fusion.43 = f32[256,4096]{1,0:T(8,128)} fusion(bf16[4096,256]{1,0:T(8,128)(2,1)S(1)} %bitcast.172, f32[256,256]{1,0:T(8,128)S(1)} %copy.166, f32[256,256]{1,0:T(8,128)S(1)} %copy.165, f32[128,256]{1,0:T(8,128)S(1)} %concatenate.37, f32[128,256]{1,0:T(8,128)S(1)} %copy.163, f32[256]{0:T(256)S(1)} %copy-done.30, f32[256]{0:T(256)S(1)} %copy-done.31, ...), kind=kOutput, calls=%fused_computation.87 | convolution fusion | flops 1074528256 | bytes 11274496 | tf_op jit(solution)/shard_map/dot_general | solution.py:245
  322.9 84.5 %reduce-scatter.2.cloned.1.call-done = f32[16,4096]{1,0:T(8,128)} async-done(((f32[256,4096]{1,0:T(8,128)}), f32[16,4096]{1,0:T(8,128)}) %reduce-scatter.2.cloned.1.call-update) | async-done | bytes 262160 | tf_op jit(solution)/shard_map/reduce_scatter | solution.py:244
  (211 shorter events, 95.0 us)
Async XLA Ops:
  7.2 159.3 %copy-start = (bf16[4096,128]{1,0:T(8,128)(2,1)S(1)}, bf16[4096,128]{1,0:T(8,128)(2,1)}, u32[]{:S(2)}) copy-start(bf16[4096,128]{1,0:T(8,128)(2,1)} %param.30) | copy-start | bytes 3145732
  7.2 91.1 %all-gather.5.cloned.1.call-start = ((), (), s32[]{:S(2)}) async-start(), calls=%async_computation.3 | async-start | bytes 5570560 | tf_op jit(solution)/shard_map/all_gather | solution.py:166
  12.4 193.4 %all-gather.7.cloned.1.call-start = ((), (), s32[]{:S(2)}) async-start(), calls=%async_computation.4 | async-start | bytes 15728640 | tf_op jit(solution)/shard_map/all_gather | solution.py:166
  99.1 2.1 collective-permute-start
  102.7 37.8 %all-to-all-start = ((bf16[16,257,256]{2,1,0:T(8,128)(2,1)}), bf16[16,257,256]{2,1,0:T(8,128)(2,1)S(1)}, u32[]{:S(2)}, u32[]{:S(2)}) async-start(bf16[16,257,256]{2,1,0:T(8,128)(2,1)} %stack.14), calls=%async_computation | async-start | bytes 4325376 | tf_op jit(solution)/shard_map/all_to_all | solution.py:148
  109.9 297.5 %reduce-scatter.2.cloned.1.call-start = ((), (), s32[]{:S(2)}) async-start(), calls=%async_computation.2 | async-start | bytes 4456448 | tf_op jit(solution)/shard_map/reduce_scatter | solution.py:244
  169.8 10.5 %collective-permute-start.1 = (f32[4,64]{1,0:T(4,128)S(1)}, f32[4,64]{1,0:T(4,128)S(1)}, u32[]{:S(2)}, u32[]{:S(2)}) collective-permute-start(f32[4,64]{1,0:T(4,128)S(1)} %reduce_sum.48), channel_id=1, source_target_pairs={{0,16},{16,32},{32,48},{48,64},{64,80},{80,96},{96,112},{112,128},... | collective-permute-start | bytes 3080 | tf_op jit(solution)/shard_map/ppermute | solution.py:18
  180.9 5.9 %collective-permute-start.2 = (f32[4,64]{1,0:T(4,128)S(1)}, f32[4,64]{1,0:T(4,128)S(1)}, u32[]{:S(2)}, u32[]{:S(2)}) collective-permute-start(f32[4,64]{1,0:T(4,128)S(1)} %get-tuple-element.134), channel_id=1, source_target_pairs={{0,16},{16,32},{32,48},{48,64},{64,80},{80,96},{96,112},{112,128},... | collective-permute-start | bytes 3080 | tf_op jit(solution)/shard_map/ppermute | solution.py:18
  186.7 24.9 %copy-start.7 = (f32[2,64,4,64]{3,2,1,0:T(4,128)}, f32[2,64,4,64]{3,2,1,0:T(4,128)S(1)}, u32[]{:S(2)}) copy-start(f32[2,64,4,64]{3,2,1,0:T(4,128)S(1)} %copy.153) | copy-start | bytes 393220
  186.8 4.3 %collective-permute-start.3 = (f32[4,64]{1,0:T(4,128)S(1)}, f32[4,64]{1,0:T(4,128)S(1)}, u32[]{:S(2)}, u32[]{:S(2)}) collective-permute-start(f32[4,64]{1,0:T(4,128)S(1)} %get-tuple-element.132), channel_id=1, source_target_pairs={{0,32},{16,48},{32,64},{48,80},{64,96},{80,112},{96,128},{112,144}... | collective-permute-start | bytes 3080 | tf_op jit(solution)/shard_map/ppermute | solution.py:18
  190.0 21.7 %copy-start.13 = (f32[2,64,4,64]{3,2,1,0:T(4,128)}, f32[2,64,4,64]{3,2,1,0:T(4,128)S(1)}, u32[]{:S(2)}) copy-start(f32[2,64,4,64]{3,2,1,0:T(4,128)S(1)} %fusion.40) | copy-start | bytes 393220
  191.1 7.4 %collective-permute-start.4 = (f32[4,64]{1,0:T(4,128)S(1)}, f32[4,64]{1,0:T(4,128)S(1)}, u32[]{:S(2)}, u32[]{:S(2)}) collective-permute-start(f32[4,64]{1,0:T(4,128)S(1)} %get-tuple-element.130), channel_id=1, source_target_pairs={{0,64},{16,80},{32,96},{48,112},{64,128},{80,144},{96,160},{112,17... | collective-permute-start | bytes 3080 | tf_op jit(solution)/shard_map/ppermute | solution.py:18
  198.5 45.2 %collective-permute-start.5 = (f32[4,64]{1,0:T(4,128)S(1)}, f32[4,64]{1,0:T(4,128)S(1)}, u32[]{:S(2)}, u32[]{:S(2)}) collective-permute-start(f32[4,64]{1,0:T(4,128)S(1)} %get-tuple-element.128), channel_id=1, source_target_pairs={{0,128},{16,144},{32,160},{48,176},{64,192},{80,208},{96,224},{112... | collective-permute-start | bytes 3080 | tf_op jit(solution)/shard_map/ppermute | solution.py:18
  223.5 25.6 %copy-start.26 = (f32[2,64]{1,0:T(2,128)S(1)}, f32[2,64]{1,0:T(2,128)}, u32[]{:S(2)}) copy-start(f32[2,64]{1,0:T(2,128)} %get-tuple-element.164) | copy-start | bytes 1540
  242.3 16.4 %copy-start.24 = (pred[64,64]{1,0:T(8,128)(4,1)S(1)}, pred[64,64]{1,0:T(8,128)(4,1)}, u32[]{:S(2)}) copy-start(pred[64,64]{1,0:T(8,128)(4,1)} %iota_compare_fusion.1) | copy-start | bytes 12292
  242.3 3.8 collective-permute-start.6
  247.0 4.2 %collective-permute-start.7 = (f32[4,64,64]{2,1,0:T(8,128)S(1)}, f32[4,64,64]{2,1,0:T(8,128)S(1)}, u32[]{:S(2)}, u32[]{:S(2)}) collective-permute-start(f32[4,64,64]{2,1,0:T(8,128)S(1)} %broadcast_select_fusion), channel_id=1, source_target_pairs={{0,16},{16,32},{32,48},{48,64},{64,80},{80,96},{96,112},{112,128},... | collective-permute-start | bytes 196616 | tf_op jit(solution)/shard_map/ppermute | solution.py:18
  251.9 10.2 %collective-permute-start.8 = (f32[4,64,64]{2,1,0:T(8,128)}, f32[4,64,64]{2,1,0:T(8,128)}, u32[]{:S(2)}, u32[]{:S(2)}) collective-permute-start(f32[4,64,64]{2,1,0:T(8,128)} %add_select_fusion.4), channel_id=1, source_target_pairs={{0,32},{16,48},{32,64},{48,80},{64,96},{80,112},{96,128},{112,144}... | collective-permute-start | bytes 196616 | tf_op jit(solution)/shard_map/ppermute | solution.py:18
  259.2 41.4 %copy-start.6 = (f32[128,4,64]{2,1,0:T(4,128)S(1)}, f32[128,4,64]{2,1,0:T(4,128)}, u32[]{:S(2)}) copy-start(f32[128,4,64]{2,1,0:T(4,128)} %copy.148) | copy-start | bytes 393220
  263.3 6.8 %collective-permute-start.9 = (f32[4,64,64]{2,1,0:T(8,128)S(1)}, f32[4,64,64]{2,1,0:T(8,128)S(1)}, u32[]{:S(2)}, u32[]{:S(2)}) collective-permute-start(f32[4,64,64]{2,1,0:T(8,128)S(1)} %add_select_fusion.3), channel_id=1, source_target_pairs={{0,64},{16,80},{32,96},{48,112},{64,128},{80,144},{96,160},{112,17... | collective-permute-start | bytes 196616 | tf_op jit(solution)/shard_map/ppermute | solution.py:18
  270.8 14.8 %collective-permute-start.10 = (f32[4,64,64]{2,1,0:T(8,128)}, f32[4,64,64]{2,1,0:T(8,128)}, u32[]{:S(2)}, u32[]{:S(2)}) collective-permute-start(f32[4,64,64]{2,1,0:T(8,128)} %add_select_fusion.2), channel_id=1, source_target_pairs={{0,128},{16,144},{32,160},{48,176},{64,192},{80,208},{96,224},{112... | collective-permute-start | bytes 196616 | tf_op jit(solution)/shard_map/ppermute | solution.py:18
  286.7 22.7 %copy-start.11 = (f32[4,64,64]{2,1,0:T(8,128)}, f32[4,64,64]{2,1,0:T(8,128)S(1)}, u32[]{:S(2)}) copy-start(f32[4,64,64]{2,1,0:T(8,128)S(1)} %add_select_fusion.1) | copy-start | bytes 196612
  286.7 22.7 %collective-permute-start.11 = (f32[4,64,64]{2,1,0:T(8,128)S(1)}, f32[4,64,64]{2,1,0:T(8,128)}, u32[]{:S(2)}, u32[]{:S(2)}) collective-permute-start(f32[4,64,64]{2,1,0:T(8,128)S(1)} %add_select_fusion.1), channel_id=1, source_target_pairs={{0,256},{16,272},{32,288},{48,304},{64,320},{80,336},{96,352},{112... | collective-permute-start | bytes 196616 | tf_op jit(solution)/shard_map/ppermute | solution.py:18
  318.4 90.6 %copy-start.1 = (bf16[4096,128]{1,0:T(8,128)(2,1)S(1)}, bf16[4096,128]{1,0:T(8,128)(2,1)}, u32[]{:S(2)}) copy-start(bf16[4096,128]{1,0:T(8,128)(2,1)} %param.30) | copy-start | bytes 3145732
  (25 other events, 103.2 us)
Sparse Core Ops, SparseCore 0:
  12.5 85.6 all-gather.4
  100.3 29.2 all-gather.6
  318.6 88.7 reduce-scatter.1
